TPU v7x, 256 devices: a whole 4x4x8 slice. The times are simulated.
256 devices in a mesh: band: 16 (over z, x_hi), fft: 16 (over x_lo, y, core).
Axes of the slice: x: 4 (x_hi: 2, x_lo: 2; x = x_hi * 2 + x_lo), y: 4, z: 8, core: 2. Of those that a mesh axis runs over, the one named last changes fastest.
Arguments:
- orbitals: bfloat16 [32, 128, 128, 128], P('band', 'fft'), may hold values from -6 to 6
- owner_order: int32 [2], replicated, may hold values from 0 to 15, as said below
- sphere_mask: int32 [128, 128, 128], P(None, 'fft'), may hold values from 0 to 1, as said below
Outputs:
- fock_images: float32 [32, 128, 128, 128], P('band', 'fft')
Inputs may be any that keep to these rules, and one draw needn't show every extreme that they name: `owner_order`: the 2 owner groups are all different, and group 16 - 1 owns one of the rounds. `sphere_mask`: zero wherever q of the steps is less than the square of 56.
All inputs are finite; a program needn't handle non-finite values.
Results may differ from a plain program's by a relative error of at most 0.018.
Values may be sent and summed in bfloat16 or wider, within the bound.
A program may use at most 64 MiB of HBM per device.

v0:
```python
import math

import jax
import jax.numpy as jnp
from jax import lax
from jax.sharding import PartitionSpec as P

ROUNDS = 2


def spread(block, axis, source):
    block = jnp.where(lax.axis_index(axis) == source, block, jnp.zeros_like(block))
    return lax.psum(block, axis)


def dft_tables(points):
    rows_index = lax.broadcasted_iota(jnp.int32, (points, points), 0)
    cols_index = lax.broadcasted_iota(jnp.int32, (points, points), 1)
    phases = 2.0 * math.pi / points * (rows_index * cols_index % points).astype(jnp.float32)
    cosine = jnp.cos(phases)
    sine = jnp.sin(phases)
    forward_x = jnp.concatenate(
        [jnp.concatenate([cosine, -sine], 1), jnp.concatenate([sine, cosine], 1)], 0
    )
    inverse_x = jnp.concatenate(
        [jnp.concatenate([cosine, sine], 1), jnp.concatenate([-sine, cosine], 1)], 0
    )
    stacked = jnp.concatenate([cosine, sine], 0)
    return (
        forward_x.astype(jnp.bfloat16),
        inverse_x.astype(jnp.bfloat16),
        stacked.astype(jnp.bfloat16),
    )


def coulomb_slab(sphere_mask):
    points = sphere_mask.shape[0]
    width = sphere_mask.shape[1]
    shape = sphere_mask.shape
    along_z = lax.broadcasted_iota(jnp.int32, shape, 0)
    along_y = lax.broadcasted_iota(jnp.int32, shape, 1) + lax.axis_index("fft") * width
    along_x = lax.broadcasted_iota(jnp.int32, shape, 2)

    def signed(values):
        return jnp.where(values < points // 2, values, values - points)

    freq_z, freq_y, freq_x = (signed(along_z), signed(along_y), signed(along_x))
    total_sq = freq_z * freq_z + freq_y * freq_y + freq_x * freq_x
    inverse = jnp.where(
        total_sq > 0, 1.0 / jnp.maximum(total_sq, 1).astype(jnp.float32), jnp.float32(0.0)
    )
    return sphere_mask.astype(jnp.float32) * inverse * jnp.float32(1.0 / (3.0 * float(points)))


def combine_parts(cos_part, sin_part, direction):
    halfway = cos_part.shape[-1] // 2
    real_part = cos_part[..., :halfway] + direction * sin_part[..., halfway:]
    imag_part = cos_part[..., halfway:] - direction * sin_part[..., :halfway]
    return jnp.concatenate([real_part, imag_part], axis=-1)


def along_rows(values_in, stacked, direction):
    points = stacked.shape[1]
    result = jnp.einsum("ay,fzyc->fzac", stacked, values_in, preferred_element_type=jnp.float32)
    return combine_parts(result[:, :, :points], result[:, :, points:], direction)


def along_columns(values_in, stacked, direction):
    points = stacked.shape[1]
    result = jnp.einsum("az,fzmc->famc", stacked, values_in, preferred_element_type=jnp.float32)
    return combine_parts(result[:, :points], result[:, points:], direction)


def respond_many(first_ones, second_ones, locals_in, tables, kernel, outward, return_trip):
    forward_x, inverse_x, stacked = tables
    points = kernel.shape[-1]
    count = locals_in.shape[0]
    packs = first_ones.shape[0]
    local_values = locals_in.astype(jnp.float32)[:, None]
    firsts = first_ones.astype(jnp.float32)[None]
    seconds = second_ones.astype(jnp.float32)[None]
    packed = jnp.concatenate(
        [
            (firsts * local_values).astype(jnp.bfloat16),
            (seconds * local_values).astype(jnp.bfloat16),
        ],
        axis=-1,
    )
    packed = packed.reshape((count * packs,) + packed.shape[2:])
    section_one = jnp.dot(packed, forward_x, preferred_element_type=jnp.float32).astype(
        jnp.bfloat16
    )
    section_two = along_rows(section_one, stacked, 1.0).astype(jnp.bfloat16)
    columns_data = outward(section_two)
    spectrum = along_columns(columns_data, stacked, 1.0)
    split_shape = spectrum.shape[:3] + (2, points)
    section_three = (
        (spectrum.reshape(split_shape) * kernel[:, :, None, :])
        .reshape(spectrum.shape)
        .astype(jnp.bfloat16)
    )
    section_four = along_columns(section_three, stacked, -1.0).astype(jnp.bfloat16)
    planes_data = return_trip(section_four)
    section_five = along_rows(planes_data, stacked, -1.0).astype(jnp.bfloat16)
    section_six = jnp.dot(section_five, inverse_x, preferred_element_type=jnp.float32)
    section_six = section_six.reshape((count, packs) + section_six.shape[1:])
    return -jnp.sum(
        firsts * section_six[..., :points] + seconds * section_six[..., points:], axis=1
    )


def shards(orbitals, owner_order, sphere_mask):
    points = orbitals.shape[-1]
    tables = dft_tables(points)
    kernel = coulomb_slab(sphere_mask)
    owner_list = []
    for round_index in range(ROUNDS):
        owner_list.append(spread(orbitals, "band", owner_order[round_index]))

    def outward(values_in):
        return lax.all_to_all(values_in, "fft", split_axis=2, concat_axis=1, tiled=True)

    def return_trip(values_in):
        return lax.all_to_all(values_in, "fft", split_axis=1, concat_axis=2, tiled=True)

    accumulated = jnp.zeros(orbitals.shape, jnp.float32)
    for round_index in range(ROUNDS):
        owner_rows = owner_list[round_index]
        first_ones = owner_rows[0::2]
        second_ones = owner_rows[1::2]

        def band_step(carry, local):
            return (
                carry,
                respond_many(
                    first_ones, second_ones, local[None], tables, kernel, outward, return_trip
                )[0],
            )

        unused, contributions = lax.scan(band_step, None, orbitals)
        accumulated = accumulated + contributions
    return accumulated


def solution(mesh):
    placed = (P("band", "fft", None, None), P(), P(None, "fft", None))
    return jax.shard_map(
        shards, mesh=mesh, in_specs=placed, out_specs=P("band", "fft", None, None), check_vma=False
    )
```

profile of v0, /device:TPU:97, one launch (start us, length us, event | category | flops | bytes accessed | tf_op | source)
XLA Modules:
  0.0 338.9 jit_solution(6651478727574558865)
XLA Ops:
  9.1 2.1 broadcast_select_fusion
  13.2 149.5 %all-reduce.3.cloned.1.call-done = (bf16[2,8,128,128]{3,2,1,0:T(8,128)(2,1)}, bf16[2,8,128,128]{3,2,1,0:T(8,128)(2,1)}) async-done(((bf16[2,8,128,128]{3,2,1,0:T(8,128)(2,1)}, bf16[2,8,128,128]{3,2,1,0:T(8,128)(2,1)}), (bf16[2,8,128,128]{3,2,1,0:T(8,128)(2,1)}, bf16[2,8,128,128]{3,2,1,0:T(8,128)(2,1)})) %all-reduce.3.cloned.1.call-update) | async-done | bytes 1048592 | tf_op jit(solution)/shard_map/psum | solution.py:13
  165.0 88.1 %while.21 = (s32[]{:T(128)}, f32[2,8,128,128]{3,2,1,0:T(8,128)}, bf16[1,8,128,128]{3,2,1,0:T(8,128)(2,1)S(1)}, bf16[2,8,128,128]{3,2,1,0:T(8,128)(2,1)}, bf16[1,...) while((s32[]{:T(128)}, f32[2,8,128,128]{3,2,1,0:T(8,128)}, ...), condition=%wide.region_5.6_spmd, body=%wide.region_4.5_spmd.sunk | while | flops 814612480 | bytes 49021216 | solution.py:140
  165.0 2.0 fusion.159
  167.0 1.9 convolution_bitcast_fusion.25
  169.5 25.7 %all_to_all.57 = bf16[1,8,128,256]{3,1,0,2:T(8,128)(2,1)S(1)} all-to-all(bf16[1,8,128,256]{3,1,0,2:T(8,128)(2,1)S(1)} %copy.87), channel_id=1, replica_groups=mesh['band'=16,'fft'=16] {'fft'}, dimensions={2} | all-to-all | bytes 1048576 | tf_op jit(solution)/shard_map/while/body/eval_jaxpr/all_to_all | solution.py:121
  197.9 4.5 %all-to-all-start.3 = ((bf16[1,128,8,256]{3,2,0,1:T(8,128)(2,1)}), bf16[1,128,8,256]{3,2,0,1:T(8,128)(2,1)S(1)}, u32[]{:S(2)}, u32[]{:S(2)}) async-start(bf16[1,128,8,256]{3,2,0,1:T(8,128)(2,1)} %copy.90), calls=%async_computation.3 | async-start | bytes 1048576 | tf_op jit(solution)/shard_map/while/body/eval_jaxpr/all_to_all | solution.py:124
  202.4 9.9 %all-to-all-done.3 = bf16[1,128,8,256]{3,2,0,1:T(8,128)(2,1)S(1)} async-done(((bf16[1,128,8,256]{3,2,0,1:T(8,128)(2,1)}), bf16[1,128,8,256]{3,2,0,1:T(8,128)(2,1)S(1)}, u32[]{:S(2)}, u32[]{:S(2)}) %all-to-all-start.3) | async-done | bytes 524320 | tf_op jit(solution)/shard_map/while/body/eval_jaxpr/all_to_all | solution.py:124
  215.2 2.0 fusion.159
  217.1 1.9 convolution_bitcast_fusion.25
  219.6 13.5 %all_to_all.57 = bf16[1,8,128,256]{3,1,0,2:T(8,128)(2,1)S(1)} all-to-all(bf16[1,8,128,256]{3,1,0,2:T(8,128)(2,1)S(1)} %copy.87), channel_id=1, replica_groups=mesh['band'=16,'fft'=16] {'fft'}, dimensions={2} | all-to-all | bytes 1048576 | tf_op jit(solution)/shard_map/while/body/eval_jaxpr/all_to_all | solution.py:121
  235.8 4.5 %all-to-all-start.3 = ((bf16[1,128,8,256]{3,2,0,1:T(8,128)(2,1)}), bf16[1,128,8,256]{3,2,0,1:T(8,128)(2,1)S(1)}, u32[]{:S(2)}, u32[]{:S(2)}) async-start(bf16[1,128,8,256]{3,2,0,1:T(8,128)(2,1)} %copy.90), calls=%async_computation.3 | async-start | bytes 1048576 | tf_op jit(solution)/shard_map/while/body/eval_jaxpr/all_to_all | solution.py:124
  240.4 9.9 %all-to-all-done.3 = bf16[1,128,8,256]{3,2,0,1:T(8,128)(2,1)S(1)} async-done(((bf16[1,128,8,256]{3,2,0,1:T(8,128)(2,1)}), bf16[1,128,8,256]{3,2,0,1:T(8,128)(2,1)S(1)}, u32[]{:S(2)}, u32[]{:S(2)}) %all-to-all-start.3) | async-done | bytes 524320 | tf_op jit(solution)/shard_map/while/body/eval_jaxpr/all_to_all | solution.py:124
  254.2 75.2 %while.20 = (s32[]{:T(128)}, f32[2,8,128,128]{3,2,1,0:T(8,128)}, bf16[1,8,128,128]{3,2,1,0:T(8,128)(2,1)S(1)}, bf16[2,8,128,128]{3,2,1,0:T(8,128)(2,1)}, bf16[1,...) while((s32[]{:T(128)}, f32[2,8,128,128]{3,2,1,0:T(8,128)}, ...), condition=%wide.region_2.3_spmd, body=%wide.region_1.2_spmd.sunk | while | flops 814612480 | bytes 46924008 | solution.py:140
  254.2 1.8 fusion.142
  256.0 1.8 convolution_bitcast_fusion.20
  258.4 13.5 %all_to_all.56 = bf16[1,8,128,256]{3,1,0,2:T(8,128)(2,1)S(1)} all-to-all(bf16[1,8,128,256]{3,1,0,2:T(8,128)(2,1)S(1)} %copy.81), channel_id=1, replica_groups=mesh['band'=16,'fft'=16] {'fft'}, dimensions={2} | all-to-all | bytes 1048576 | tf_op jit(solution)/shard_map/while/body/eval_jaxpr/all_to_all | solution.py:121
  274.6 4.5 %all-to-all-start.1 = ((bf16[1,128,8,256]{3,2,0,1:T(8,128)(2,1)}), bf16[1,128,8,256]{3,2,0,1:T(8,128)(2,1)S(1)}, u32[]{:S(2)}, u32[]{:S(2)}) async-start(bf16[1,128,8,256]{3,2,0,1:T(8,128)(2,1)} %copy.84), calls=%async_computation.1 | async-start | bytes 1048576 | tf_op jit(solution)/shard_map/while/body/eval_jaxpr/all_to_all | solution.py:124
  279.1 9.9 %all-to-all-done.1 = bf16[1,128,8,256]{3,2,0,1:T(8,128)(2,1)S(1)} async-done(((bf16[1,128,8,256]{3,2,0,1:T(8,128)(2,1)}), bf16[1,128,8,256]{3,2,0,1:T(8,128)(2,1)S(1)}, u32[]{:S(2)}, u32[]{:S(2)}) %all-to-all-start.1) | async-done | bytes 524320 | tf_op jit(solution)/shard_map/while/body/eval_jaxpr/all_to_all | solution.py:124
  293.6 1.8 convolution_bitcast_fusion.20
  296.0 13.5 %all_to_all.56 = bf16[1,8,128,256]{3,1,0,2:T(8,128)(2,1)S(1)} all-to-all(bf16[1,8,128,256]{3,1,0,2:T(8,128)(2,1)S(1)} %copy.81), channel_id=1, replica_groups=mesh['band'=16,'fft'=16] {'fft'}, dimensions={2} | all-to-all | bytes 1048576 | tf_op jit(solution)/shard_map/while/body/eval_jaxpr/all_to_all | solution.py:121
  312.2 4.5 %all-to-all-start.1 = ((bf16[1,128,8,256]{3,2,0,1:T(8,128)(2,1)}), bf16[1,128,8,256]{3,2,0,1:T(8,128)(2,1)S(1)}, u32[]{:S(2)}, u32[]{:S(2)}) async-start(bf16[1,128,8,256]{3,2,0,1:T(8,128)(2,1)} %copy.84), calls=%async_computation.1 | async-start | bytes 1048576 | tf_op jit(solution)/shard_map/while/body/eval_jaxpr/all_to_all | solution.py:124
  316.8 9.9 %all-to-all-done.1 = bf16[1,128,8,256]{3,2,0,1:T(8,128)(2,1)S(1)} async-done(((bf16[1,128,8,256]{3,2,0,1:T(8,128)(2,1)}), bf16[1,128,8,256]{3,2,0,1:T(8,128)(2,1)S(1)}, u32[]{:S(2)}, u32[]{:S(2)}) %all-to-all-start.1) | async-done | bytes 524320 | tf_op jit(solution)/shard_map/while/body/eval_jaxpr/all_to_all | solution.py:124
  329.4 2.6 add.91
  (115 shorter events, 32.6 us)
Async XLA Ops:
  6.5 4.7 %copy-start.8 = (s32[128,8,128]{2,1,0:T(8,128)S(1)}, s32[128,8,128]{2,1,0:T(8,128)}, u32[]{:S(2)}) copy-start(s32[128,8,128]{2,1,0:T(8,128)} %param.9) | copy-start | bytes 1572868
  6.5 156.2 %all-reduce.3.cloned.1.call-start = ((), (), s32[]{:S(2)}) async-start(), calls=%async_computation.4 | async-start | bytes 2097152 | tf_op jit(solution)/shard_map/psum | solution.py:13
  165.0 2.0 copy-start
  197.9 14.4 %all-to-all-start.3 = ((bf16[1,128,8,256]{3,2,0,1:T(8,128)(2,1)}), bf16[1,128,8,256]{3,2,0,1:T(8,128)(2,1)S(1)}, u32[]{:S(2)}, u32[]{:S(2)}) async-start(bf16[1,128,8,256]{3,2,0,1:T(8,128)(2,1)} %copy.90), calls=%async_computation.3 | async-start | bytes 1048576 | tf_op jit(solution)/shard_map/while/body/eval_jaxpr/all_to_all | solution.py:124
  212.3 0.9 copy-start.2
  212.8 1.0 copy-start.1
  212.8 1.3 copy-start.6
  214.2 1.0 copy-start.7
  215.2 2.0 copy-start
  235.8 14.4 %all-to-all-start.3 = ((bf16[1,128,8,256]{3,2,0,1:T(8,128)(2,1)}), bf16[1,128,8,256]{3,2,0,1:T(8,128)(2,1)S(1)}, u32[]{:S(2)}, u32[]{:S(2)}) async-start(bf16[1,128,8,256]{3,2,0,1:T(8,128)(2,1)} %copy.90), calls=%async_computation.3 | async-start | bytes 1048576 | tf_op jit(solution)/shard_map/while/body/eval_jaxpr/all_to_all | solution.py:124
  250.3 0.9 copy-start.2
  250.7 1.0 copy-start.1
  250.7 1.3 copy-start.6
  252.2 1.0 copy-start.7
  274.6 14.4 %all-to-all-start.1 = ((bf16[1,128,8,256]{3,2,0,1:T(8,128)(2,1)}), bf16[1,128,8,256]{3,2,0,1:T(8,128)(2,1)S(1)}, u32[]{:S(2)}, u32[]{:S(2)}) async-start(bf16[1,128,8,256]{3,2,0,1:T(8,128)(2,1)} %copy.84), calls=%async_computation.1 | async-start | bytes 1048576 | tf_op jit(solution)/shard_map/while/body/eval_jaxpr/all_to_all | solution.py:124
  289.0 0.9 copy-start.3
  289.5 1.2 copy-start.4
  290.9 1.0 copy-start.5
  312.2 14.4 %all-to-all-start.1 = ((bf16[1,128,8,256]{3,2,0,1:T(8,128)(2,1)}), bf16[1,128,8,256]{3,2,0,1:T(8,128)(2,1)S(1)}, u32[]{:S(2)}, u32[]{:S(2)}) async-start(bf16[1,128,8,256]{3,2,0,1:T(8,128)(2,1)} %copy.84), calls=%async_computation.1 | async-start | bytes 1048576 | tf_op jit(solution)/shard_map/while/body/eval_jaxpr/all_to_all | solution.py:124
  326.6 0.9 copy-start.3
  327.1 1.2 copy-start.4
  328.5 1.0 copy-start.5
Sparse Core Ops, SparseCore 0:
  11.4 151.2 all-reduce.2
where the time goes:
time: 342 us; the launch traced here: 339 us
  waiting for transfers between devices  189 us (55%)
  blocking collectives  66.1 us (19%)
  local copies, waits for them, and re-layouts  18.9 us (6%)
  starting transfers between devices  18.1 us (5%)
  other arithmetic  17.3 us (5%)
  between operations  14.8 us (4%)
  matrix products  14.2 us (4%)
    psum x1, waiting for transfers between devices, spread(): return lax.psum(block, axis)  150 us
    all_to_all x4, blocking collectives, outward(): lax.all_to_all(values_in, 'fft', split_axis=2, concat_axis=1, tiled=True)  66.1 us
    all_to_all x4, waiting for transfers between devices, return_trip(): lax.all_to_all(values_in, 'fft', split_axis=1, concat_axis=2, tiled=True)  39.5 us
    all_to_all x4, starting transfers between devices, return_trip(): lax.all_to_all(values_in, 'fft', split_axis=1, concat_axis=2, tiled=True)  18.1 us
    dot_general x8, matrix products, along_rows(): jnp.einsum('ay,fzyc->fzac', stacked, values_in, preferred_element_type=jn...  9.2 us
    convert_element_type x4, other arithmetic, respond_many(): (firsts * local_values).astype(jnp.bfloat16)  7.5 us
    while x32, local copies, waits for them, and re-layouts  6.97 us
  transfers between devices with their start and end apart: 5, of which 5 were waited for; matrix products, arithmetic and copies ran while one was open for 1% of the time, Pallas kernels for 0%

commit v1 on v0

v1 whole, which is shorter than its diff:
```python
import functools
import math

import jax
import jax.numpy as jnp
import ml_dtypes
import numpy as np
from jax import lax
from jax.experimental import pallas as pl
from jax.experimental.pallas import tpu as pltpu
from jax.sharding import PartitionSpec as P

MESH = pl.DeviceIdType.MESH
N = 128
NZ = 8
NF = 16
F32 = jnp.float32
BF16 = jnp.bfloat16


def dft_tables():
    k = np.arange(N)
    phases = 2.0 * math.pi / N * ((k[:, None] * k[None, :]) % N)
    c, s = np.cos(phases), np.sin(phases)
    forward = np.block([[c, s], [-s, c]])
    inverse = np.block([[c, -s], [s, c]])
    pairs = np.arange(2 * N).reshape(2, N).T.reshape(-1)
    tables = (
        forward.T,
        inverse.T,
        forward,
        inverse,
        forward[:, pairs],
        inverse[pairs, :],
    )
    return np.stack(tables).astype(ml_dtypes.bfloat16)


def body(
    order_ref, orb_ref, mask_ref, tab_ref, out_ref,
    own15, owng, masked, parts, partial, half,
    kern, rows_f32, out_send, out_land, ret_send, ret_land,
    send_sem, land_sem, cast_send, cast_land,
    scatter_send, scatter_land, gather_send, gather_land, cross_send, cross_land, local_sem,
):
    band = lax.axis_index("band")
    f = lax.axis_index("fft")
    z = band // 2
    xh = band % 2

    barrier = pltpu.get_barrier_semaphore()

    def greet(device):
        pl.semaphore_signal(barrier, inc=1, device_id=device, device_id_type=MESH)

    def z_peer(k):
        return (((z + k) % NZ) * 2 + xh, f)

    across = (z * 2 + 1 - xh, f)

    @pl.loop(1, NF)
    def _(k):
        greet((band, (f + k) % NF))

    @pl.loop(1, NZ)
    def _(k):
        greet(z_peer(k))

    greet(across)

    def signed(v):
        return jnp.where(v < N // 2, v, v - N)

    @pl.loop(0, 8)
    def _(k):
        along_z = signed(lax.broadcasted_iota(jnp.int32, (N, N), 0))
        along_x = signed(lax.broadcasted_iota(jnp.int32, (N, N), 1))
        along_y = signed(f * 8 + k)
        total = along_z * along_z + along_x * along_x + along_y * along_y
        inverse = jnp.where(total > 0, 1.0 / jnp.maximum(total, 1).astype(F32), F32(0.0))
        bits = mask_ref[pl.ds(k, N, stride=8), :].astype(F32)
        kern[k] = bits * inverse * F32(1.0 / (3.0 * N))

    other = jnp.minimum(order_ref[0], order_ref[1])

    @pl.loop(0, 8)
    def _(p):
        for o in range(2):
            value = orb_ref[o, p]
            masked[p, o] = jnp.where(other == band, value, jnp.zeros_like(value))

    pl.semaphore_wait(barrier, NF - 1 + NZ - 1 + 1)

    def cast_copy(p, way, device):
        return pltpu.make_async_remote_copy(
            src_ref=own15.at[p], dst_ref=own15.at[p],
            send_sem=cast_send.at[way, p], recv_sem=cast_land.at[p],
            device_id=device, device_id_type=MESH,
        )

    root = (z == NZ - 1) & (xh == 1)
    up = (z == NZ - 1) | (z < 3)
    down = z > 4
    to_up = (((z + 1) % NZ) * 2 + xh, f)
    to_down = (((z + NZ - 1) % NZ) * 2 + xh, f)

    def forward_cast(p):
        @pl.when(up)
        def _():
            cast_copy(p, 0, to_up).start()

        @pl.when(down)
        def _():
            cast_copy(p, 1, to_down).start()

        @pl.when(root)
        def _():
            cast_copy(p, 2, across).start()

    def out_copy(unit, j):
        return pltpu.make_async_remote_copy(
            src_ref=out_send.at[unit, j], dst_ref=out_land.at[unit, f],
            send_sem=send_sem.at[0, unit, j], recv_sem=land_sem.at[0, unit, f],
            device_id=(band, j), device_id_type=MESH,
        )

    def out_wait(unit, j):
        pltpu.make_async_remote_copy(
            src_ref=out_send.at[unit, j], dst_ref=out_land.at[unit, j],
            send_sem=send_sem.at[0, unit, j], recv_sem=land_sem.at[0, unit, j],
            device_id=(band, j), device_id_type=MESH,
        ).wait_recv()

    def ret_copy(unit, j):
        return pltpu.make_async_remote_copy(
            src_ref=ret_send.at[unit, j], dst_ref=ret_land.at[unit, f],
            send_sem=send_sem.at[1, unit, j], recv_sem=land_sem.at[1, unit, f],
            device_id=(band, j), device_id_type=MESH,
        )

    def ret_wait(unit, j):
        pltpu.make_async_remote_copy(
            src_ref=ret_send.at[unit, j], dst_ref=ret_land.at[unit, j],
            send_sem=send_sem.at[1, unit, j], recv_sem=land_sem.at[1, unit, j],
            device_id=(band, j), device_id_type=MESH,
        ).wait_recv()

    def scatter_copy(k):
        t = (z + k) % NZ
        return pltpu.make_async_remote_copy(
            src_ref=masked.at[t], dst_ref=parts.at[k],
            send_sem=scatter_send.at[k], recv_sem=scatter_land.at[k],
            device_id=(t * 2 + xh, f), device_id_type=MESH,
        )

    def cross_copy():
        return pltpu.make_async_remote_copy(
            src_ref=partial, dst_ref=half, send_sem=cross_send, recv_sem=cross_land,
            device_id=across, device_id_type=MESH,
        )

    def gather_copy(k):
        t = (z + k) % NZ
        return pltpu.make_async_remote_copy(
            src_ref=parts.at[0], dst_ref=owng.at[z],
            send_sem=gather_send.at[k], recv_sem=gather_land.at[z],
            device_id=(t * 2 + xh, f), device_id_type=MESH,
        )

    def gather_wait(p):
        pltpu.make_async_remote_copy(
            src_ref=parts.at[0], dst_ref=owng.at[p],
            send_sem=gather_send.at[0], recv_sem=gather_land.at[p],
            device_id=across, device_id_type=MESH,
        ).wait_recv()

    def transform_planes(owner, local, first):
        dens = []
        for i in range(2):
            p = first + i
            mine = orb_ref[local, p]
            dens.append(jnp.concatenate([owner[p, 0] * mine, owner[p, 1] * mine], axis=1))
        one = jnp.dot(jnp.concatenate(dens, axis=0), tab_ref[0], preferred_element_type=F32)
        one = one.astype(BF16)
        right = jnp.concatenate(
            [
                jnp.concatenate([one[:N, :N], one[N:, :N]], axis=1),
                jnp.concatenate([one[:N, N:], one[N:, N:]], axis=1),
            ],
            axis=0,
        )
        two = jnp.dot(tab_ref[2], right, preferred_element_type=F32)
        for i in range(2):
            start = pl.multiple_of((first + i) * 2 * N, 2 * N)
            rows_f32[local, pl.ds(start, 2 * N), :] = two[:, i * N : (i + 1) * N]

    def send_out(unit, local):
        @pl.loop(0, NF)
        def _(k):
            j = (f + k) % NF
            for i in range(8):
                tile = rows_f32[local, pl.ds(j * 8 + i, 16, stride=N), :]
                out_send[unit, j, i] = tile.astype(BF16)

            @pl.when(k > 0)
            def _():
                out_copy(unit, j).start()

            @pl.when(k == 0)
            def _():
                pltpu.make_async_copy(
                    out_send.at[unit, j], out_land.at[unit, j], local_sem.at[0, unit]
                ).start()

    def spectrum(unit):
        pltpu.make_async_copy(
            out_send.at[unit, f], out_land.at[unit, f], local_sem.at[0, unit]
        ).wait()

        @pl.loop(1, NF)
        def _(k):
            out_wait(unit, (f + k) % NF)

        @pl.loop(0, 4)
        def _(pair):
            cols = [out_land[unit, :, pair * 2 + i].reshape(2 * N, N) for i in range(2)]
            three = jnp.dot(
                tab_ref[4], jnp.concatenate(cols, axis=1), preferred_element_type=F32
            )
            weights = jnp.concatenate([kern[pair * 2], kern[pair * 2 + 1]], axis=1)
            weights = jnp.concatenate([weights, weights], axis=0)
            three = (three * weights).astype(BF16)
            four = jnp.dot(tab_ref[5], three, preferred_element_type=F32).astype(BF16)
            for i in range(2):
                ret_send[unit, :, pair * 2 + i] = four[:, i * N : (i + 1) * N].reshape(NF, 16, N)

        pltpu.make_async_copy(
            ret_send.at[unit, f], ret_land.at[unit, f], local_sem.at[1, unit]
        ).start()

        @pl.loop(1, NF)
        def _(k):
            ret_copy(unit, (f + k) % NF).start()

    def images(unit, owner, local, fresh):
        pltpu.make_async_copy(
            ret_send.at[unit, f], ret_land.at[unit, f], local_sem.at[1, unit]
        ).wait()

        @pl.loop(0, NF)
        def _(k):
            j = (f + k) % NF

            @pl.when(k > 0)
            def _():
                ret_wait(unit, j)

            value = ret_land[unit, j].astype(F32).reshape(N, N)
            rows_f32[local, pl.ds(pl.multiple_of(j * N, N), N), :] = value

        @pl.loop(0, 4)
        def _(pair):
            first = pair * 2
            planes = []
            for i in range(2):
                row = (first + i) * 2
                re = rows_f32[local, pl.ds(row, N, stride=16), :].astype(BF16)
                im = rows_f32[local, pl.ds(row + 1, N, stride=16), :].astype(BF16)
                planes.append(jnp.concatenate([re, im], axis=0))
            five = jnp.dot(
                tab_ref[3], jnp.concatenate(planes, axis=1), preferred_element_type=F32
            ).astype(BF16)
            left = jnp.concatenate(
                [
                    jnp.concatenate([five[:N, :N], five[N:, :N]], axis=1),
                    jnp.concatenate([five[:N, N:], five[N:, N:]], axis=1),
                ],
                axis=0,
            )
            six = jnp.dot(left, tab_ref[1], preferred_element_type=F32)
            for i in range(2):
                p = first + i
                pot = six[i * N : (i + 1) * N]
                term = owner[p, 0].astype(F32) * pot[:, :N] + owner[p, 1].astype(F32) * pot[:, N:]
                if fresh:
                    out_ref[local, p] = -term
                else:
                    out_ref[local, p] = out_ref[local, p] - term

    def local_cast(p):
        return pltpu.make_async_copy(orb_ref.at[:, p], own15.at[p], cast_land.at[p])

    @pl.when(root)
    def _():
        @pl.loop(0, 8)
        def _(p):
            local_cast(p).start()

    @pl.loop(0, 4)
    def _(pair):
        for i in range(2):
            p = pair * 2 + i

            @pl.when(root)
            def _():
                local_cast(p).wait()

            @pl.when(jnp.logical_not(root))
            def _():
                cast_copy(p, 0, across).wait_recv()

            forward_cast(p)
        for local in range(2):
            transform_planes(own15, local, pair * 2)

    @pl.loop(1, NZ)
    def _(k):
        scatter_copy(k).start()

    for local in range(2):
        send_out(local, local)
    spectrum(0)

    parts[0] = masked[z]

    @pl.loop(1, NZ)
    def _(k):
        scatter_copy(k).wait_recv()
        parts[0] = parts[0] + parts[k]

    partial[...] = parts[0]
    cross_copy().start()
    spectrum(1)
    cross_copy().wait()
    parts[0] = partial[...] + half[...]
    owng[z] = parts[0]

    @pl.loop(1, NZ)
    def _(k):
        gather_copy(k).start()

    @pl.loop(1, NZ)
    def _(k):
        gather_wait((z + k) % NZ)

    for local in range(2):
        @pl.loop(0, 4)
        def _(pair):
            transform_planes(owng, local, pair * 2)

        send_out(2 + local, local)

    for local in range(2):
        images(local, own15, local, True)
    for local in range(2):
        spectrum(2 + local)
    for local in range(2):
        images(2 + local, owng, local, False)

    @pl.loop(0, 8)
    def _(p):
        @pl.when(up)
        def _():
            cast_copy(p, 0, to_up).wait_send()

        @pl.when(down)
        def _():
            cast_copy(p, 1, to_down).wait_send()

        @pl.when(root)
        def _():
            cast_copy(p, 2, across).wait_send()

    @pl.loop(1, NZ)
    def _(k):
        scatter_copy(k).wait_send()
        gather_copy(k).wait_send()

    @pl.loop(0, 4)
    def _(unit):
        @pl.loop(1, NF)
        def _(k):
            out_copy(unit, (f + k) % NF).wait_send()
            ret_copy(unit, (f + k) % NF).wait_send()


def shards(orbitals, owner_order, sphere_mask):
    tables = jnp.asarray(dft_tables())
    mask_rows = sphere_mask.reshape(N * 8, N)
    vmem = pl.BlockSpec(memory_space=pltpu.VMEM)
    dma = pltpu.SemaphoreType.DMA
    plane = (2, N, N)
    return pl.pallas_call(
        body,
        name="exchange",
        out_shape=jax.ShapeDtypeStruct(orbitals.shape, F32),
        in_specs=[pl.BlockSpec(memory_space=pltpu.SMEM), vmem, vmem, vmem],
        out_specs=vmem,
        scratch_shapes=[
            pltpu.VMEM((8,) + plane, BF16),
            pltpu.VMEM((8,) + plane, BF16),
            pltpu.VMEM((8,) + plane, BF16),
            pltpu.VMEM((NZ,) + plane, BF16),
            pltpu.VMEM(plane, BF16),
            pltpu.VMEM(plane, BF16),
            pltpu.VMEM((8, N, N), F32),
            pltpu.VMEM((2, 16 * N, N), F32),
            pltpu.VMEM((4, NF, 8, 16, N), BF16),
            pltpu.VMEM((4, NF, 8, 16, N), BF16),
            pltpu.VMEM((4, NF, 8, 16, N), BF16),
            pltpu.VMEM((4, NF, 8, 16, N), BF16),
            dma((2, 4, NF)),
            dma((2, 4, NF)),
            dma((3, 8)),
            dma((8,)),
            dma((NZ,)),
            dma((NZ,)),
            dma((NZ,)),
            dma((8,)),
            dma(()),
            dma(()),
            dma((2, 4)),
        ],
        compiler_params=pltpu.CompilerParams(
            collective_id=0, has_side_effects=True, vmem_limit_bytes=60 * 1024 * 1024
        ),
    )(owner_order, orbitals, mask_rows, tables)


def solution(mesh):
    placed = (P("band", "fft", None, None), P(), P(None, "fft", None))
    return jax.shard_map(
        shards, mesh=mesh, in_specs=placed, out_specs=P("band", "fft", None, None), check_vma=False
    )
```

time: 342 us -> 111 us (0.32)
  the two profiles are of different devices: /device:TPU:97 before, /device:TPU:215 now
where the time goes in v1:
time: 111 us
  Pallas kernels  109 us (98%)
  local copies, waits for them, and re-layouts  2.3 us (2%)
    pallas_call x1, Pallas kernels, shards(): pl.pallas_call(body, name='exchange', out_shape=jax.ShapeDtypeStruct(orbi...  109 us
    unnamed x1, local copies, waits for them, and re-layouts  2.3 us

profile of v1, /device:TPU:215, one launch (start us, length us, event | category | flops | bytes accessed | tf_op | source)
XLA Modules:
  0.0 111.4 jit_solution(6092905816065240462)
XLA Ops:
  0.0 109.0 %exchange.1 = f32[2,8,128,128]{3,2,1,0:T(8,128)} custom-call(s32[2]{0:T(128)} %order_ref.1, bf16[2,8,128,128]{3,2,1,0:T(8,128)(2,1)} %orb_ref.1, s32[1024,128]{1,0:T(8,128)} %bitcast.1, bf16[6,256,256]{2,1,0:T(8,128)(2,1)} %constant.2.clone.tab_ref), custom_call_target="tpu_custom_call" | custom-call | tf_op jit(solution)/shard_map/exchange/pallas_call | solution.py:393
  109.1 2.3 %copy.6 = f32[2,8,128,128]{3,2,1,0:T(8,128)} copy(f32[2,8,128,128]{3,2,1,0:T(8,128)} %exchange.1) | data formatting | bytes 2097152

commit v2 on v1

--- a/solution.py
+++ b/solution.py
@@ -16,6 +16,9 @@
 NF = 16
 F32 = jnp.float32
 BF16 = jnp.bfloat16
+CUTS = 2
+PIECE = N // CUTS
+LAG = 2
 
 
 def dft_tables():
@@ -89,33 +92,69 @@
             value = orb_ref[o, p]
             masked[p, o] = jnp.where(other == band, value, jnp.zeros_like(value))
 
+    @pl.when((z == NZ - 1) & (xh == 1))
+    def _():
+        @pl.loop(0, 8)
+        def _(p):
+            for o in range(2):
+                own15[p, o] = orb_ref[o, p]
+
     pl.semaphore_wait(barrier, NF - 1 + NZ - 1 + 1)
-
-    def cast_copy(p, way, device):
-        return pltpu.make_async_remote_copy(
-            src_ref=own15.at[p], dst_ref=own15.at[p],
-            send_sem=cast_send.at[way, p], recv_sem=cast_land.at[p],
-            device_id=device, device_id_type=MESH,
-        )
 
     root = (z == NZ - 1) & (xh == 1)
     up = (z == NZ - 1) | (z < 3)
     down = z > 4
     to_up = (((z + 1) % NZ) * 2 + xh, f)
     to_down = (((z + NZ - 1) % NZ) * 2 + xh, f)
-
-    def forward_cast(p):
+    shares = (z < NZ - 1) | (xh == 1)
+
+    def piece(q, o):
+        return own15.at[q // CUTS, o, pl.ds(pl.multiple_of((q % CUTS) * PIECE, PIECE), PIECE)]
+
+    def cast_copy(q, way, o, lands, device):
+        return pltpu.make_async_remote_copy(
+            src_ref=piece(q, o), dst_ref=piece(q, o),
+            send_sem=cast_send.at[way, q], recv_sem=cast_land.at[lands, q],
+            device_id=device, device_id_type=MESH,
+        )
+
+    def cast_up(q):
+        return cast_copy(q, 0, 1 - xh, 0, to_up)
+
+    def cast_down(q):
+        return cast_copy(q, 1, 1 - xh, 0, to_down)
+
+    def cast_share(q):
+        return cast_copy(q, 2, 1 - xh, 1, across)
+
+    def cast_first(q):
+        return cast_copy(q, 3, xh, 0, across)
+
+    def pass_on(q):
+        @pl.when(jnp.logical_not(root))
+        def _():
+            cast_up(q).wait_recv()
+
+        @pl.when(root)
+        def _():
+            cast_first(q).start()
+
         @pl.when(up)
         def _():
-            cast_copy(p, 0, to_up).start()
+            cast_up(q).start()
 
         @pl.when(down)
         def _():
-            cast_copy(p, 1, to_down).start()
-
-        @pl.when(root)
-        def _():
-            cast_copy(p, 2, across).start()
+            cast_down(q).start()
+
+        @pl.when(shares)
+        def _():
+            cast_share(q).start()
+
+    def shared(q):
+        @pl.when(jnp.logical_not(root))
+        def _():
+            cast_copy(q, 2, xh, 1, across).wait_recv()
 
     def out_copy(unit, j):
         return pltpu.make_async_remote_copy(
@@ -287,50 +326,42 @@
                 else:
                     out_ref[local, p] = out_ref[local, p] - term
 
-    def local_cast(p):
-        return pltpu.make_async_copy(orb_ref.at[:, p], own15.at[p], cast_land.at[p])
-
-    @pl.when(root)
-    def _():
-        @pl.loop(0, 8)
-        def _(p):
-            local_cast(p).start()
-
-    @pl.loop(0, 4)
-    def _(pair):
-        for i in range(2):
-            p = pair * 2 + i
-
-            @pl.when(root)
-            def _():
-                local_cast(p).wait()
-
-            @pl.when(jnp.logical_not(root))
-            def _():
-                cast_copy(p, 0, across).wait_recv()
-
-            forward_cast(p)
-        for local in range(2):
-            transform_planes(own15, local, pair * 2)
+    per_pair = 2 * CUTS
 
     @pl.loop(1, NZ)
     def _(k):
         scatter_copy(k).start()
 
+    @pl.loop(0, 4 + LAG)
+    def _(step):
+        @pl.when(step < 4)
+        def _():
+            @pl.loop(0, per_pair)
+            def _(i):
+                pass_on(step * per_pair + i)
+
+        @pl.when(step >= LAG)
+        def _():
+            pair = step - LAG
+
+            @pl.loop(0, per_pair)
+            def _(i):
+                shared(pair * per_pair + i)
+
+            for local in range(2):
+                transform_planes(own15, local, pair * 2)
+
+    parts[0] = masked[z]
+
+    @pl.loop(1, NZ)
+    def _(k):
+        scatter_copy(k).wait_recv()
+        parts[0] = parts[0] + parts[k]
+
+    partial[...] = parts[0]
+    cross_copy().start()
     for local in range(2):
         send_out(local, local)
-    spectrum(0)
-
-    parts[0] = masked[z]
-
-    @pl.loop(1, NZ)
-    def _(k):
-        scatter_copy(k).wait_recv()
-        parts[0] = parts[0] + parts[k]
-
-    partial[...] = parts[0]
-    cross_copy().start()
-    spectrum(1)
     cross_copy().wait()
     parts[0] = partial[...] + half[...]
     owng[z] = parts[0]
@@ -338,6 +369,9 @@
     @pl.loop(1, NZ)
     def _(k):
         gather_copy(k).start()
+
+    spectrum(0)
+    spectrum(1)
 
     @pl.loop(1, NZ)
     def _(k):
@@ -357,19 +391,23 @@
     for local in range(2):
         images(2 + local, owng, local, False)
 
-    @pl.loop(0, 8)
-    def _(p):
+    @pl.loop(0, 8 * CUTS)
+    def _(q):
         @pl.when(up)
         def _():
-            cast_copy(p, 0, to_up).wait_send()
+            cast_up(q).wait_send()
 
         @pl.when(down)
         def _():
-            cast_copy(p, 1, to_down).wait_send()
+            cast_down(q).wait_send()
+
+        @pl.when(shares)
+        def _():
+            cast_share(q).wait_send()
 
         @pl.when(root)
         def _():
-            cast_copy(p, 2, across).wait_send()
+            cast_first(q).wait_send()
 
     @pl.loop(1, NZ)
     def _(k):
@@ -411,8 +449,8 @@
             pltpu.VMEM((4, NF, 8, 16, N), BF16),
             dma((2, 4, NF)),
             dma((2, 4, NF)),
-            dma((3, 8)),
-            dma((8,)),
+            dma((4, 8 * CUTS)),
+            dma((2, 8 * CUTS)),
             dma((NZ,)),
             dma((NZ,)),
             dma((NZ,)),

time: 111 us -> 99.3 us (0.89)
  the two profiles are of different devices: /device:TPU:215 before, /device:TPU:97 now
where the time goes in v2:
time: 99.3 us; the launch traced here: 99 us
  Pallas kernels  96.7 us (97%)
  local copies, waits for them, and re-layouts  2.3 us (2%)
    pallas_call x1, Pallas kernels, shards(): pl.pallas_call(body, name='exchange', out_shape=jax.ShapeDtypeStruct(orbi...  96.7 us
    unnamed x1, local copies, waits for them, and re-layouts  2.3 us

profile of v2, /device:TPU:97, one launch (start us, length us, event | category | flops | bytes accessed | tf_op | source)
XLA Modules:
  0.0 99.0 jit_solution(12343583437603249911)
XLA Ops:
  0.0 96.7 %exchange.1 = f32[2,8,128,128]{3,2,1,0:T(8,128)} custom-call(s32[2]{0:T(128)} %order_ref.1, bf16[2,8,128,128]{3,2,1,0:T(8,128)(2,1)} %orb_ref.1, s32[1024,128]{1,0:T(8,128)} %bitcast.1, bf16[6,256,256]{2,1,0:T(8,128)(2,1)} %constant.2.clone.tab_ref), custom_call_target="tpu_custom_call" | custom-call | tf_op jit(solution)/shard_map/exchange/pallas_call | solution.py:431
  96.7 2.3 %copy.6 = f32[2,8,128,128]{3,2,1,0:T(8,128)} copy(f32[2,8,128,128]{3,2,1,0:T(8,128)} %exchange.1) | data formatting | bytes 2097152

commit v3 on v2

--- a/solution.py
+++ b/solution.py
@@ -19,6 +19,7 @@
 CUTS = 2
 PIECE = N // CUTS
 LAG = 2
+LATE_AT = 3
 
 
 def dft_tables():
@@ -33,17 +34,21 @@
         inverse.T,
         forward,
         inverse,
-        forward[:, pairs],
         inverse[pairs, :],
     )
-    return np.stack(tables).astype(ml_dtypes.bfloat16)
+    z_half = forward.reshape(2 * N, 2, NF, 2, 4).transpose(0, 3, 2, 4, 1)
+    wide = np.zeros((2, 2 * N, 2, NF, 2, 4, 2))
+    for k in range(2):
+        wide[k, :, :, :, k] = z_half
+    wide = wide.reshape(4 * N, 4 * N)
+    return np.stack(tables).astype(ml_dtypes.bfloat16), wide.astype(ml_dtypes.bfloat16)
 
 
 def body(
-    order_ref, orb_ref, mask_ref, tab_ref, out_ref,
+    order_ref, orb_ref, mask_ref, tab_ref, wide_ref, out_ref,
     own15, owng, masked, parts, partial, half,
     kern, rows_f32, out_send, out_land, ret_send, ret_land,
-    send_sem, land_sem, cast_send, cast_land,
+    out_send_sem, out_land_sem, send_sem, land_sem, cast_send, cast_land,
     scatter_send, scatter_land, gather_send, gather_land, cross_send, cross_land, local_sem,
 ):
     band = lax.axis_index("band")
@@ -102,8 +107,8 @@
     pl.semaphore_wait(barrier, NF - 1 + NZ - 1 + 1)
 
     root = (z == NZ - 1) & (xh == 1)
-    up = (z == NZ - 1) | (z < 3)
-    down = z > 4
+    up = (z == NZ - 1) | (z < 2)
+    down = z > 3
     to_up = (((z + 1) % NZ) * 2 + xh, f)
     to_down = (((z + NZ - 1) % NZ) * 2 + xh, f)
     shares = (z < NZ - 1) | (xh == 1)
@@ -114,7 +119,7 @@
     def cast_copy(q, way, o, lands, device):
         return pltpu.make_async_remote_copy(
             src_ref=piece(q, o), dst_ref=piece(q, o),
-            send_sem=cast_send.at[way, q], recv_sem=cast_land.at[lands, q],
+            send_sem=cast_send.at[way], recv_sem=cast_land.at[lands, q],
             device_id=device, device_id_type=MESH,
         )
 
@@ -135,10 +140,6 @@
         def _():
             cast_up(q).wait_recv()
 
-        @pl.when(root)
-        def _():
-            cast_first(q).start()
-
         @pl.when(up)
         def _():
             cast_up(q).start()
@@ -156,31 +157,40 @@
         def _():
             cast_copy(q, 2, xh, 1, across).wait_recv()
 
-    def out_copy(unit, j):
-        return pltpu.make_async_remote_copy(
-            src_ref=out_send.at[unit, j], dst_ref=out_land.at[unit, f],
-            send_sem=send_sem.at[0, unit, j], recv_sem=land_sem.at[0, unit, f],
+    def out_copy(unit, c, j):
+        return pltpu.make_async_remote_copy(
+            src_ref=out_send.at[unit, c, j], dst_ref=out_land.at[unit, c, f],
+            send_sem=out_send_sem.at[unit, c], recv_sem=out_land_sem.at[unit, c],
             device_id=(band, j), device_id_type=MESH,
         )
 
-    def out_wait(unit, j):
-        pltpu.make_async_remote_copy(
-            src_ref=out_send.at[unit, j], dst_ref=out_land.at[unit, j],
-            send_sem=send_sem.at[0, unit, j], recv_sem=land_sem.at[0, unit, j],
-            device_id=(band, j), device_id_type=MESH,
-        ).wait_recv()
+    def out_all(unit, c):
+        rest = pl.ds(0, NF - 1)
+        return pltpu.make_async_remote_copy(
+            src_ref=out_send.at[unit, c, rest], dst_ref=out_land.at[unit, c, rest],
+            send_sem=out_send_sem.at[unit, c], recv_sem=out_land_sem.at[unit, c],
+            device_id=across, device_id_type=MESH,
+        )
+
+    def ret_all(unit):
+        rest = pl.ds(0, NF - 1)
+        return pltpu.make_async_remote_copy(
+            src_ref=ret_send.at[unit, rest], dst_ref=ret_land.at[unit, rest],
+            send_sem=send_sem.at[unit], recv_sem=land_sem.at[unit, 0],
+            device_id=across, device_id_type=MESH,
+        )
 
     def ret_copy(unit, j):
         return pltpu.make_async_remote_copy(
             src_ref=ret_send.at[unit, j], dst_ref=ret_land.at[unit, f],
-            send_sem=send_sem.at[1, unit, j], recv_sem=land_sem.at[1, unit, f],
+            send_sem=send_sem.at[unit], recv_sem=land_sem.at[unit, f],
             device_id=(band, j), device_id_type=MESH,
         )
 
     def ret_wait(unit, j):
         pltpu.make_async_remote_copy(
             src_ref=ret_send.at[unit, j], dst_ref=ret_land.at[unit, j],
-            send_sem=send_sem.at[1, unit, j], recv_sem=land_sem.at[1, unit, j],
+            send_sem=send_sem.at[unit], recv_sem=land_sem.at[unit, j],
             device_id=(band, j), device_id_type=MESH,
         ).wait_recv()
 
@@ -188,7 +198,7 @@
         t = (z + k) % NZ
         return pltpu.make_async_remote_copy(
             src_ref=masked.at[t], dst_ref=parts.at[k],
-            send_sem=scatter_send.at[k], recv_sem=scatter_land.at[k],
+            send_sem=scatter_send, recv_sem=scatter_land,
             device_id=(t * 2 + xh, f), device_id_type=MESH,
         )
 
@@ -202,16 +212,24 @@
         t = (z + k) % NZ
         return pltpu.make_async_remote_copy(
             src_ref=parts.at[0], dst_ref=owng.at[z],
-            send_sem=gather_send.at[k], recv_sem=gather_land.at[z],
+            send_sem=gather_send, recv_sem=gather_land,
             device_id=(t * 2 + xh, f), device_id_type=MESH,
         )
 
-    def gather_wait(p):
-        pltpu.make_async_remote_copy(
-            src_ref=parts.at[0], dst_ref=owng.at[p],
-            send_sem=gather_send.at[0], recv_sem=gather_land.at[p],
+    def scatter_rest():
+        return pltpu.make_async_remote_copy(
+            src_ref=masked.at[pl.ds(0, NZ - 1)], dst_ref=parts.at[pl.ds(1, NZ - 1)],
+            send_sem=scatter_send, recv_sem=scatter_land,
             device_id=across, device_id_type=MESH,
-        ).wait_recv()
+        )
+
+    def gather_rest():
+        rest = pl.ds(0, NZ - 1)
+        return pltpu.make_async_remote_copy(
+            src_ref=parts.at[rest], dst_ref=owng.at[rest],
+            send_sem=gather_send, recv_sem=gather_land,
+            device_id=across, device_id_type=MESH,
+        )
 
     def transform_planes(owner, local, first):
         dens = []
@@ -233,48 +251,53 @@
             start = pl.multiple_of((first + i) * 2 * N, 2 * N)
             rows_f32[local, pl.ds(start, 2 * N), :] = two[:, i * N : (i + 1) * N]
 
-    def send_out(unit, local):
+    def send_out(unit, local, c):
         @pl.loop(0, NF)
         def _(k):
             j = (f + k) % NF
-            for i in range(8):
-                tile = rows_f32[local, pl.ds(j * 8 + i, 16, stride=N), :]
-                out_send[unit, j, i] = tile.astype(BF16)
+            for i in range(4):
+                row = c * 8 * N + j * 8 + i * 2
+                tiles = [
+                    rows_f32[local, pl.ds(row + ky, 8, stride=N), :] for ky in range(2)
+                ]
+                out_send[unit, c, j, i] = jnp.concatenate(tiles, axis=0).astype(BF16)
 
             @pl.when(k > 0)
             def _():
-                out_copy(unit, j).start()
+                out_copy(unit, c, j).start()
 
             @pl.when(k == 0)
             def _():
                 pltpu.make_async_copy(
-                    out_send.at[unit, j], out_land.at[unit, j], local_sem.at[0, unit]
+                    out_send.at[unit, c, j], out_land.at[unit, c, j], local_sem.at[c, unit]
                 ).start()
 
     def spectrum(unit):
+        for c in range(2):
+            pltpu.make_async_copy(
+                out_send.at[unit, c, f], out_land.at[unit, c, f], local_sem.at[c, unit]
+            ).wait()
+
+            out_all(unit, c).wait_recv()
+
+        @pl.loop(0, 2)
+        def _(quad):
+            cols = [out_land[unit, :, :, quad * 2 + i].reshape(4 * N, N) for i in range(2)]
+            three = jnp.dot(
+                wide_ref[...], jnp.concatenate(cols, axis=1), preferred_element_type=F32
+            )
+            for ky in range(2):
+                first = quad * 4 + ky
+                weights = jnp.concatenate([kern[first], kern[first + 2]], axis=1)
+                weights = jnp.concatenate([weights, weights], axis=0)
+                part = (three[ky * 2 * N : (ky + 1) * 2 * N] * weights).astype(BF16)
+                four = jnp.dot(tab_ref[4], part, preferred_element_type=F32).astype(BF16)
+                for i in range(2):
+                    block = four[:, i * N : (i + 1) * N].reshape(NF, 16, N)
+                    ret_send[unit, :, first + 2 * i] = block
+
         pltpu.make_async_copy(
-            out_send.at[unit, f], out_land.at[unit, f], local_sem.at[0, unit]
-        ).wait()
-
-        @pl.loop(1, NF)
-        def _(k):
-            out_wait(unit, (f + k) % NF)
-
-        @pl.loop(0, 4)
-        def _(pair):
-            cols = [out_land[unit, :, pair * 2 + i].reshape(2 * N, N) for i in range(2)]
-            three = jnp.dot(
-                tab_ref[4], jnp.concatenate(cols, axis=1), preferred_element_type=F32
-            )
-            weights = jnp.concatenate([kern[pair * 2], kern[pair * 2 + 1]], axis=1)
-            weights = jnp.concatenate([weights, weights], axis=0)
-            three = (three * weights).astype(BF16)
-            four = jnp.dot(tab_ref[5], three, preferred_element_type=F32).astype(BF16)
-            for i in range(2):
-                ret_send[unit, :, pair * 2 + i] = four[:, i * N : (i + 1) * N].reshape(NF, 16, N)
-
-        pltpu.make_async_copy(
-            ret_send.at[unit, f], ret_land.at[unit, f], local_sem.at[1, unit]
+            ret_send.at[unit, f], ret_land.at[unit, f], local_sem.at[2, unit]
         ).start()
 
         @pl.loop(1, NF)
@@ -283,7 +306,7 @@
 
     def images(unit, owner, local, fresh):
         pltpu.make_async_copy(
-            ret_send.at[unit, f], ret_land.at[unit, f], local_sem.at[1, unit]
+            ret_send.at[unit, f], ret_land.at[unit, f], local_sem.at[2, unit]
         ).wait()
 
         @pl.loop(0, NF)
@@ -328,9 +351,20 @@
 
     per_pair = 2 * CUTS
 
+    @pl.when(root)
+    def _():
+        @pl.loop(0, 8 * CUTS)
+        def _(q):
+            cast_first(q).start()
+
+    def free_route(k):
+        return jnp.where(k < 4, (z >= 2) & (z + k <= NZ - 1), (k > 4) & (z <= 3) & (z + k >= NZ - 1))
+
     @pl.loop(1, NZ)
     def _(k):
-        scatter_copy(k).start()
+        @pl.when(free_route(k))
+        def _():
+            scatter_copy(k).start()
 
     @pl.loop(0, 4 + LAG)
     def _(step):
@@ -351,17 +385,27 @@
             for local in range(2):
                 transform_planes(own15, local, pair * 2)
 
-    parts[0] = masked[z]
+            @pl.when(pair % 2 == 1)
+            def _():
+                for local in range(2):
+                    send_out(local, local, pair // 2)
+
+        @pl.when(step == LATE_AT)
+        def _():
+            @pl.loop(1, NZ)
+            def _(k):
+                @pl.when(jnp.logical_not(free_route(k)))
+                def _():
+                    scatter_copy(k).start()
+
+    scatter_rest().wait_recv()
+    partial[...] = masked[z]
 
     @pl.loop(1, NZ)
     def _(k):
-        scatter_copy(k).wait_recv()
-        parts[0] = parts[0] + parts[k]
-
-    partial[...] = parts[0]
+        partial[...] = partial[...] + parts[k]
+
     cross_copy().start()
-    for local in range(2):
-        send_out(local, local)
     cross_copy().wait()
     parts[0] = partial[...] + half[...]
     owng[z] = parts[0]
@@ -373,16 +417,16 @@
     spectrum(0)
     spectrum(1)
 
-    @pl.loop(1, NZ)
-    def _(k):
-        gather_wait((z + k) % NZ)
+    gather_rest().wait_recv()
 
     for local in range(2):
         @pl.loop(0, 4)
         def _(pair):
             transform_planes(owng, local, pair * 2)
 
-        send_out(2 + local, local)
+            @pl.when(pair % 2 == 1)
+            def _():
+                send_out(2 + local, local, pair // 2)
 
     for local in range(2):
         images(local, own15, local, True)
@@ -391,39 +435,41 @@
     for local in range(2):
         images(2 + local, owng, local, False)
 
-    @pl.loop(0, 8 * CUTS)
-    def _(q):
-        @pl.when(up)
-        def _():
-            cast_up(q).wait_send()
-
-        @pl.when(down)
-        def _():
-            cast_down(q).wait_send()
-
-        @pl.when(shares)
-        def _():
-            cast_share(q).wait_send()
-
-        @pl.when(root)
-        def _():
-            cast_first(q).wait_send()
-
-    @pl.loop(1, NZ)
-    def _(k):
-        scatter_copy(k).wait_send()
-        gather_copy(k).wait_send()
+    def cast_left(way, o):
+        pltpu.make_async_remote_copy(
+            src_ref=own15.at[:, o], dst_ref=own15.at[:, o],
+            send_sem=cast_send.at[way], recv_sem=cast_land.at[0, 0],
+            device_id=across, device_id_type=MESH,
+        ).wait_send()
+
+    @pl.when(up)
+    def _():
+        cast_left(0, 1 - xh)
+
+    @pl.when(down)
+    def _():
+        cast_left(1, 1 - xh)
+
+    @pl.when(shares)
+    def _():
+        cast_left(2, 1 - xh)
+
+    @pl.when(root)
+    def _():
+        cast_left(3, xh)
+
+    scatter_rest().wait_send()
+    gather_rest().wait_send()
 
     @pl.loop(0, 4)
     def _(unit):
-        @pl.loop(1, NF)
-        def _(k):
-            out_copy(unit, (f + k) % NF).wait_send()
-            ret_copy(unit, (f + k) % NF).wait_send()
+        for c in range(2):
+            out_all(unit, c).wait_send()
+        ret_all(unit).wait_send()
 
 
 def shards(orbitals, owner_order, sphere_mask):
-    tables = jnp.asarray(dft_tables())
+    tables, wide = (jnp.asarray(table) for table in dft_tables())
     mask_rows = sphere_mask.reshape(N * 8, N)
     vmem = pl.BlockSpec(memory_space=pltpu.VMEM)
     dma = pltpu.SemaphoreType.DMA
@@ -432,7 +478,7 @@
         body,
         name="exchange",
         out_shape=jax.ShapeDtypeStruct(orbitals.shape, F32),
-        in_specs=[pl.BlockSpec(memory_space=pltpu.SMEM), vmem, vmem, vmem],
+        in_specs=[pl.BlockSpec(memory_space=pltpu.SMEM)] + [vmem] * 4,
         out_specs=vmem,
         scratch_shapes=[
             pltpu.VMEM((8,) + plane, BF16),
@@ -443,26 +489,28 @@
             pltpu.VMEM(plane, BF16),
             pltpu.VMEM((8, N, N), F32),
             pltpu.VMEM((2, 16 * N, N), F32),
+            pltpu.VMEM((4, 2, NF, 4, 16, N), BF16),
+            pltpu.VMEM((4, 2, NF, 4, 16, N), BF16),
             pltpu.VMEM((4, NF, 8, 16, N), BF16),
             pltpu.VMEM((4, NF, 8, 16, N), BF16),
-            pltpu.VMEM((4, NF, 8, 16, N), BF16),
-            pltpu.VMEM((4, NF, 8, 16, N), BF16),
-            dma((2, 4, NF)),
-            dma((2, 4, NF)),
-            dma((4, 8 * CUTS)),
+            dma((4, 2)),
+            dma((4, 2)),
+            dma((4,)),
+            dma((4, NF)),
+            dma((4,)),
             dma((2, 8 * CUTS)),
-            dma((NZ,)),
-            dma((NZ,)),
-            dma((NZ,)),
-            dma((8,)),
             dma(()),
             dma(()),
-            dma((2, 4)),
+            dma(()),
+            dma(()),
+            dma(()),
+            dma(()),
+            dma((3, 4)),
         ],
         compiler_params=pltpu.CompilerParams(
             collective_id=0, has_side_effects=True, vmem_limit_bytes=60 * 1024 * 1024
         ),
-    )(owner_order, orbitals, mask_rows, tables)
+    )(owner_order, orbitals, mask_rows, tables, wide)
 
 
 def solution(mesh):

time: 99.3 us -> 91.1 us (0.917)
  Pallas kernels: 96.7 us -> 88.7 us
    pallas_call x1, Pallas kernels: 96.7 us -> 88.7 us  [shards(): pl.pallas_call(body, name='exchange', out_shape=jax.ShapeDtypeStruct(orbi...]
where the time goes in v3:
time: 91.1 us; the launch traced here: 91 us
  Pallas kernels  88.7 us (97%)
  local copies, waits for them, and re-layouts  2.3 us (3%)
    pallas_call x1, Pallas kernels, shards(): pl.pallas_call(body, name='exchange', out_shape=jax.ShapeDtypeStruct(orbi...  88.7 us
    unnamed x1, local copies, waits for them, and re-layouts  2.3 us

profile of v3, /device:TPU:97, one launch (start us, length us, event | category | flops | bytes accessed | tf_op | source)
XLA Modules:
  0.0 91.0 jit_solution(16312715394744659861)
XLA Ops:
  0.0 88.7 %exchange.1 = f32[2,8,128,128]{3,2,1,0:T(8,128)} custom-call(s32[2]{0:T(128)} %order_ref.1, bf16[2,8,128,128]{3,2,1,0:T(8,128)(2,1)} %orb_ref.1, s32[1024,128]{1,0:T(8,128)} %bitcast.1, bf16[5,256,256]{2,1,0:T(8,128)(2,1)} %constant.4.clone.tab_ref, bf16[512,512]{1,0:T(8,128)(2,1)} %constant.5.clone.wide_ref), custom_call_target="tpu_custom_call" | custom-call | tf_op jit(solution)/shard_map/exchange/pallas_call | solution.py:477
  88.7 2.3 %copy.7 = f32[2,8,128,128]{3,2,1,0:T(8,128)} copy(f32[2,8,128,128]{3,2,1,0:T(8,128)} %exchange.1) | data formatting | bytes 2097152

commit v4 on v3

--- a/solution.py
+++ b/solution.py
@@ -176,23 +176,16 @@
         rest = pl.ds(0, NF - 1)
         return pltpu.make_async_remote_copy(
             src_ref=ret_send.at[unit, rest], dst_ref=ret_land.at[unit, rest],
-            send_sem=send_sem.at[unit], recv_sem=land_sem.at[unit, 0],
+            send_sem=send_sem.at[unit], recv_sem=land_sem.at[unit],
             device_id=across, device_id_type=MESH,
         )
 
     def ret_copy(unit, j):
         return pltpu.make_async_remote_copy(
             src_ref=ret_send.at[unit, j], dst_ref=ret_land.at[unit, f],
-            send_sem=send_sem.at[unit], recv_sem=land_sem.at[unit, f],
+            send_sem=send_sem.at[unit], recv_sem=land_sem.at[unit],
             device_id=(band, j), device_id_type=MESH,
         )
-
-    def ret_wait(unit, j):
-        pltpu.make_async_remote_copy(
-            src_ref=ret_send.at[unit, j], dst_ref=ret_land.at[unit, j],
-            send_sem=send_sem.at[unit], recv_sem=land_sem.at[unit, j],
-            device_id=(band, j), device_id_type=MESH,
-        ).wait_recv()
 
     def scatter_copy(k):
         t = (z + k) % NZ
@@ -300,8 +293,7 @@
             ret_send.at[unit, f], ret_land.at[unit, f], local_sem.at[2, unit]
         ).start()
 
-        @pl.loop(1, NF)
-        def _(k):
+        for k in range(1, NF):
             ret_copy(unit, (f + k) % NF).start()
 
     def images(unit, owner, local, fresh):
@@ -309,14 +301,10 @@
             ret_send.at[unit, f], ret_land.at[unit, f], local_sem.at[2, unit]
         ).wait()
 
+        ret_all(unit).wait_recv()
+
         @pl.loop(0, NF)
-        def _(k):
-            j = (f + k) % NF
-
-            @pl.when(k > 0)
-            def _():
-                ret_wait(unit, j)
-
+        def _(j):
             value = ret_land[unit, j].astype(F32).reshape(N, N)
             rows_f32[local, pl.ds(pl.multiple_of(j * N, N), N), :] = value
 
@@ -496,7 +484,7 @@
             dma((4, 2)),
             dma((4, 2)),
             dma((4,)),
-            dma((4, NF)),
+            dma((4,)),
             dma((4,)),
             dma((2, 8 * CUTS)),
             dma(()),

time: 91.1 us -> 90.5 us (level)
  no operation moved by 1% of the time
where the time goes in v4:
time: 90.5 us; the launch traced here: 90.3 us
  Pallas kernels  88 us (97%)
  local copies, waits for them, and re-layouts  2.3 us (3%)
    pallas_call x1, Pallas kernels, shards(): pl.pallas_call(body, name='exchange', out_shape=jax.ShapeDtypeStruct(orbi...  88 us
    unnamed x1, local copies, waits for them, and re-layouts  2.3 us

profile of v4, /device:TPU:97, one launch (start us, length us, event | category | flops | bytes accessed | tf_op | source)
XLA Modules:
  0.0 90.3 jit_solution(9056657709921391285)
XLA Ops:
  0.0 88.0 %exchange.1 = f32[2,8,128,128]{3,2,1,0:T(8,128)} custom-call(s32[2]{0:T(128)} %order_ref.1, bf16[2,8,128,128]{3,2,1,0:T(8,128)(2,1)} %orb_ref.1, s32[1024,128]{1,0:T(8,128)} %bitcast.1, bf16[5,256,256]{2,1,0:T(8,128)(2,1)} %constant.4.clone.tab_ref, bf16[512,512]{1,0:T(8,128)(2,1)} %constant.5.clone.wide_ref), custom_call_target="tpu_custom_call" | custom-call | tf_op jit(solution)/shard_map/exchange/pallas_call | solution.py:465
  88.0 2.3 %copy.7 = f32[2,8,128,128]{3,2,1,0:T(8,128)} copy(f32[2,8,128,128]{3,2,1,0:T(8,128)} %exchange.1) | data formatting | bytes 2097152

commit v5 on v4

--- a/solution.py
+++ b/solution.py
@@ -394,6 +394,7 @@
         partial[...] = partial[...] + parts[k]
 
     cross_copy().start()
+    spectrum(0)
     cross_copy().wait()
     parts[0] = partial[...] + half[...]
     owng[z] = parts[0]
@@ -402,7 +403,6 @@
     def _(k):
         gather_copy(k).start()
 
-    spectrum(0)
     spectrum(1)
 
     gather_rest().wait_recv()

time: 90.5 us -> 90 us (level)
  Pallas kernels: 88 us -> 86.8 us
    pallas_call x1, Pallas kernels: 88 us -> 86.8 us  [shards(): pl.pallas_call(body, name='exchange', out_shape=jax.ShapeDtypeStruct(orbi...]
where the time goes in v5:
time: 90 us; the launch traced here: 89.1 us
  Pallas kernels  86.8 us (96%)
  local copies, waits for them, and re-layouts  2.3 us (3%)
    pallas_call x1, Pallas kernels, shards(): pl.pallas_call(body, name='exchange', out_shape=jax.ShapeDtypeStruct(orbi...  86.8 us
    unnamed x1, local copies, waits for them, and re-layouts  2.3 us

profile of v5, /device:TPU:97, one launch (start us, length us, event | category | flops | bytes accessed | tf_op | source)
XLA Modules:
  0.0 89.1 jit_solution(7904044132339561817)
XLA Ops:
  0.0 86.8 %exchange.1 = f32[2,8,128,128]{3,2,1,0:T(8,128)} custom-call(s32[2]{0:T(128)} %order_ref.1, bf16[2,8,128,128]{3,2,1,0:T(8,128)(2,1)} %orb_ref.1, s32[1024,128]{1,0:T(8,128)} %bitcast.1, bf16[5,256,256]{2,1,0:T(8,128)(2,1)} %constant.4.clone.tab_ref, bf16[512,512]{1,0:T(8,128)(2,1)} %constant.5.clone.wide_ref), custom_call_target="tpu_custom_call" | custom-call | tf_op jit(solution)/shard_map/exchange/pallas_call | solution.py:465
  86.8 2.3 %copy.7 = f32[2,8,128,128]{3,2,1,0:T(8,128)} copy(f32[2,8,128,128]{3,2,1,0:T(8,128)} %exchange.1) | data formatting | bytes 2097152

commit v6 on v5

--- a/solution.py
+++ b/solution.py
@@ -172,6 +172,21 @@
             device_id=across, device_id_type=MESH,
         )
 
+    def whole_copy(unit, j):
+        return pltpu.make_async_remote_copy(
+            src_ref=out_send.at[unit, :, j], dst_ref=out_land.at[unit, :, f],
+            send_sem=out_send_sem.at[unit, 0], recv_sem=out_land_sem.at[unit, 0],
+            device_id=(band, j), device_id_type=MESH,
+        )
+
+    def whole_all(unit):
+        rest = pl.ds(0, NF - 1)
+        return pltpu.make_async_remote_copy(
+            src_ref=out_send.at[unit, :, rest], dst_ref=out_land.at[unit, :, rest],
+            send_sem=out_send_sem.at[unit, 0], recv_sem=out_land_sem.at[unit, 0],
+            device_id=across, device_id_type=MESH,
+        )
+
     def ret_all(unit):
         rest = pl.ds(0, NF - 1)
         return pltpu.make_async_remote_copy(
@@ -265,13 +280,39 @@
                     out_send.at[unit, c, j], out_land.at[unit, c, j], local_sem.at[c, unit]
                 ).start()
 
+    def send_whole(unit, local):
+        @pl.loop(0, NF)
+        def _(k):
+            j = (f + k) % NF
+            for c in range(2):
+                for i in range(4):
+                    row = c * 8 * N + j * 8 + i * 2
+                    tiles = [
+                        rows_f32[local, pl.ds(row + ky, 8, stride=N), :] for ky in range(2)
+                    ]
+                    out_send[unit, c, j, i] = jnp.concatenate(tiles, axis=0).astype(BF16)
+
+            @pl.when(k > 0)
+            def _():
+                whole_copy(unit, j).start()
+
+            @pl.when(k == 0)
+            def _():
+                for c in range(2):
+                    pltpu.make_async_copy(
+                        out_send.at[unit, c, j], out_land.at[unit, c, j], local_sem.at[c, unit]
+                    ).start()
+
     def spectrum(unit):
+        if unit >= 2:
+            whole_all(unit).wait_recv()
         for c in range(2):
             pltpu.make_async_copy(
                 out_send.at[unit, c, f], out_land.at[unit, c, f], local_sem.at[c, unit]
             ).wait()
 
-            out_all(unit, c).wait_recv()
+            if unit < 2:
+                out_all(unit, c).wait_recv()
 
         @pl.loop(0, 2)
         def _(quad):
@@ -412,9 +453,7 @@
         def _(pair):
             transform_planes(owng, local, pair * 2)
 
-            @pl.when(pair % 2 == 1)
-            def _():
-                send_out(2 + local, local, pair // 2)
+        send_whole(2 + local, local)
 
     for local in range(2):
         images(local, own15, local, True)
@@ -449,10 +488,12 @@
     scatter_rest().wait_send()
     gather_rest().wait_send()
 
-    @pl.loop(0, 4)
-    def _(unit):
-        for c in range(2):
-            out_all(unit, c).wait_send()
+    for unit in range(4):
+        if unit < 2:
+            for c in range(2):
+                out_all(unit, c).wait_send()
+        else:
+            whole_all(unit).wait_send()
         ret_all(unit).wait_send()
 
 

time: 90 us -> 90.8 us (level)
  no operation moved by 1% of the time
where the time goes in v6:
time: 90.8 us; the launch traced here: 89.1 us
  Pallas kernels  86.8 us (96%)
  local copies, waits for them, and re-layouts  2.3 us (3%)
    pallas_call x1, Pallas kernels, shards(): pl.pallas_call(body, name='exchange', out_shape=jax.ShapeDtypeStruct(orbi...  86.8 us
    unnamed x1, local copies, waits for them, and re-layouts  2.3 us

profile of v6, /device:TPU:97, one launch (start us, length us, event | category | flops | bytes accessed | tf_op | source)
XLA Modules:
  0.0 89.1 jit_solution(16869724427680601556)
XLA Ops:
  0.0 86.8 %exchange.1 = f32[2,8,128,128]{3,2,1,0:T(8,128)} custom-call(s32[2]{0:T(128)} %order_ref.1, bf16[2,8,128,128]{3,2,1,0:T(8,128)(2,1)} %orb_ref.1, s32[1024,128]{1,0:T(8,128)} %bitcast.1, bf16[5,256,256]{2,1,0:T(8,128)(2,1)} %constant.4.clone.tab_ref, bf16[512,512]{1,0:T(8,128)(2,1)} %constant.5.clone.wide_ref), custom_call_target="tpu_custom_call" | custom-call | tf_op jit(solution)/shard_map/exchange/pallas_call | solution.py:506
  86.8 2.3 %copy.7 = f32[2,8,128,128]{3,2,1,0:T(8,128)} copy(f32[2,8,128,128]{3,2,1,0:T(8,128)} %exchange.1) | data formatting | bytes 2097152
